TPU v7x, 256 devices: a whole 4x4x8 slice. The times are simulated.
256 devices in a mesh: row: 4 (over x), col: 16 (over z, core), depth: 4 (over y).
Axes of the slice: x: 4, y: 4, z: 8, core: 2. Of those that a mesh axis runs over, the one named last changes fastest.
Arguments:
- amplitudes: float32 [8, 768, 6144], P('depth', 'col', 'row'), may hold values from -6 to 6
- integrals: float32 [8, 768, 16, 768], P('depth', 'row', 'col'), may hold values from -0.21875 to 0.21875
- irrep_virtual: int32 [768], replicated, may hold values from 0 to 7, as said below
- irrep_first: int32 [8], replicated, may hold values from 0 to 7
- irrep_second: int32 [8], replicated, may hold values from 0 to 7
- irrep_target: int32 [16], replicated, may hold values from 0 to 7
Outputs:
- cycle_term: float32 [16, 768, 6144], P('col', 'depth', 'row')
Inputs may be any that keep to these rules, and one draw needn't show every extreme that they name: `irrep_virtual`: labels never fall along the virtual orbitals, so each irrep is one contiguous block, the blocks in rising order of irrep; every irrep holds 64 or more virtuals.
All inputs are finite; a program needn't handle non-finite values.
Results may differ from a plain program's by a relative error of at most 0.0001.
Values sent between devices are 32-bit elements; how exact they have to be, the bound alone decides.
No kernel may reach another device: no remote copies, remote signals or barrier semaphores. Data moves between devices by JAX's collectives and lax.ppermute only.
A program may use at most 64 MiB of HBM per device.

v0:
```python
import jax
import jax.numpy as jnp
from jax import lax
from jax.sharding import PartitionSpec as P


def amp_mask(labels_k, labels_c, labels_x):
    parity = jnp.bitwise_xor(
        jnp.bitwise_xor(labels_k[:, None, None], labels_c[None, :, None]), labels_x[None, None, :]
    )
    return (parity == 0).astype(jnp.float32)


def int_mask(labels_k, labels_c, labels_j, labels_b):
    parity = jnp.bitwise_xor(
        jnp.bitwise_xor(labels_k[:, None, None, None], labels_c[None, :, None, None]),
        jnp.bitwise_xor(labels_j[None, None, :, None], labels_b[None, None, None, :]),
    )
    return (parity == 0).astype(jnp.float32)


def contract(left_amp, right_int):
    return jnp.einsum(
        "kcjb,kcx->jbx",
        right_int,
        left_amp,
        precision=lax.Precision.HIGHEST,
        preferred_element_type=jnp.float32,
    )


def per_device(amplitudes, integrals, irrep_virtual, irrep_first, irrep_second, irrep_target):
    k_local = amplitudes.shape[0]
    x_local = amplitudes.shape[2]
    j_local = integrals.shape[2]
    all_x = jnp.bitwise_xor(irrep_virtual[:, None], irrep_first[None, :]).reshape(-1)
    labels_k = lax.dynamic_slice_in_dim(irrep_second, lax.axis_index("depth") * k_local, k_local)
    labels_x = lax.dynamic_slice_in_dim(all_x, lax.axis_index("row") * x_local, x_local)
    labels_j = lax.dynamic_slice_in_dim(irrep_target, lax.axis_index("col") * j_local, j_local)
    gathered = lax.all_gather(amplitudes, "col", axis=1, tiled=True)
    gathered = gathered * amp_mask(labels_k, irrep_virtual, labels_x)
    masked = lax.all_gather(integrals, "row", axis=1, tiled=True) * int_mask(
        labels_k, irrep_virtual, labels_j, irrep_virtual
    )
    partial_sum = contract(gathered, masked)
    return lax.psum_scatter(partial_sum, "depth", scatter_dimension=1, tiled=True)


def solution(mesh):
    return jax.shard_map(
        per_device,
        mesh=mesh,
        in_specs=(P("depth", "col", "row"), P("depth", "row", "col", None), P(), P(), P(), P()),
        out_specs=P("col", "depth", "row"),
        check_vma=False,
    )
```

profile of v0, /device:TPU:1, one launch (start us, length us, event | category | flops | bytes accessed | tf_op | source)
XLA Modules:
  0.0 219.6 jit_solution(11587721565921521954)
XLA Ops:
  6.5 0.0 all-gather.3.cloned.1.call-start
  6.5 0.7 all-gather.3.cloned.1.call-update
  7.3 0.0 all-gather.5.cloned.1.call-start
  7.3 0.7 all-gather.5.cloned.1.call-update
  8.0 0.0 reduce-scatter.2.cloned.1.call-start
  8.1 0.9 broadcast_xor_fusion
  8.9 0.2 xor.105
  9.1 1.2 dynamic_slice.10
  10.4 0.7 dynamic_slice.9
  11.1 0.1 dynamic_slice.11
  11.2 1.3 broadcast_xor_fusion.2
  12.5 0.8 broadcast_xor_fusion.1
  13.3 54.6 %all-gather.3.cloned.1.call-done = f32[2,768,1,768]{3,2,1,0:T(1,128)} async-done(((f32[2,192,1,768]{3,2,1,0:T(1,128)}), f32[2,768,1,768]{3,2,1,0:T(1,128)}) %all-gather.3.cloned.1.call-update) | async-done | bytes 4718608 | tf_op jit(solution)/shard_map/all_gather | solution.py:42
  67.9 8.2 %compare_select_fusion = f32[2,768,1,768]{3,2,1,0:T(1,128)} fusion(f32[2,768,1,768]{3,2,1,0:T(1,128)} %all-gather.3.cloned.1.call-done, s32[768]{0:T(1024)S(1)} %broadcast_xor_fusion.2, s32[2,768]{1,0:T(2,128)S(1)} %broadcast_xor_fusion.1), kind=kLoop, calls=%fused_computation | loop fusion | flops 3538944 | bytes 9446400 | tf_op jit(solution)/shard_map/mul | solution.py:42
  76.1 55.5 %all-gather.5.cloned.1.call-done = f32[2,768,1536]{2,1,0:T(8,128)} async-done(((f32[2,48,1536]{2,1,0:T(8,128)}), f32[2,768,1536]{2,1,0:T(8,128)}) %all-gather.5.cloned.1.call-update) | async-done | bytes 9437200 | tf_op jit(solution)/shard_map/all_gather | solution.py:40
  131.6 29.5 %fusion.8 = f32[1,768,1536]{2,1,0:T(8,128)} fusion(f32[2,768,1536]{2,1,0:T(8,128)} %all-gather.5.cloned.1.call-done, s32[1536]{0:T(1024)S(1)} %dynamic_slice.11, s32[2,768]{1,0:T(2,128)S(1)} %broadcast_xor_fusion.1, f32[2,768,1,768]{3,2,1,0:T(1,128)} %compare_select_fusion), kind=kOutput, calls=%fused_computation.10 | convolution fusion | flops 21750349824 | bytes 18886656 | tf_op jit(solution)/shard_map/kcjb,kcx->jbx/dot_general | solution.py:23
  161.1 0.0 reduce-scatter.2.cloned.1.call-update
  161.1 51.9 %reduce-scatter.2.cloned.1.call-done = f32[1,192,1536]{2,1,0:T(8,128)} async-done(((f32[1,768,1536]{2,1,0:T(8,128)}), f32[1,192,1536]{2,1,0:T(8,128)}) %reduce-scatter.2.cloned.1.call-update) | async-done | bytes 1179664 | tf_op jit(solution)/shard_map/reduce_scatter | solution.py:46
Async XLA Ops:
  6.5 61.4 %all-gather.3.cloned.1.call-start = ((), (), s32[]{:S(2)}) async-start(), calls=%async_computation.1 | async-start | bytes 5898240 | tf_op jit(solution)/shard_map/all_gather | solution.py:42
  7.3 124.3 %all-gather.5.cloned.1.call-start = ((), (), s32[]{:S(2)}) async-start(), calls=%async_computation.2 | async-start | bytes 10027008 | tf_op jit(solution)/shard_map/all_gather | solution.py:40
  8.0 205.0 %reduce-scatter.2.cloned.1.call-start = ((), (), s32[]{:S(2)}) async-start(), calls=%async_computation.3 | async-start | bytes 5898240 | tf_op jit(solution)/shard_map/reduce_scatter | solution.py:46
Sparse Core Ops, SparseCore 0:
  9.1 58.7 all-gather.2
  69.7 61.7 all-gather.4
  161.2 51.7 reduce-scatter.1
where the time goes:
time: 220 us
  waiting for transfers between devices  164 us (75%)
  matrix products  29.5 us (13%)
  between operations  13.1 us (6%)
  other arithmetic  11.1 us (5%)
  local copies, waits for them, and re-layouts  2.25 us (1%)
    all_gather x1, waiting for transfers between devices, per_device(): gathered = lax.all_gather(amplitudes, 'col', axis=1, tiled=True)  55.5 us
    all_gather x1, waiting for transfers between devices, per_device(): lax.all_gather(integrals, 'row', axis=1, tiled=True)  54.6 us
    reduce_scatter x1, waiting for transfers between devices, per_device(): lax.psum_scatter(partial_sum, 'depth', scatter_dimension=1, tiled=True)  51.9 us
    dot_general x1, matrix products, contract(): jnp.einsum('kcjb,kcx->jbx', right_int, left_amp, precision=lax.Precision....  29.5 us
    mul x1, other arithmetic, per_device(): lax.all_gather(integrals, 'row', axis=1, tiled=True)  8.17 us
  transfers between devices with their start and end apart: 3, of which 3 were waited for; matrix products, arithmetic and copies ran while one was open for 6% of the time, Pallas kernels for 0%

commit v1 on v0

--- a/solution.py
+++ b/solution.py
@@ -37,7 +37,8 @@
     labels_k = lax.dynamic_slice_in_dim(irrep_second, lax.axis_index("depth") * k_local, k_local)
     labels_x = lax.dynamic_slice_in_dim(all_x, lax.axis_index("row") * x_local, x_local)
     labels_j = lax.dynamic_slice_in_dim(irrep_target, lax.axis_index("col") * j_local, j_local)
-    gathered = lax.all_gather(amplitudes, "col", axis=1, tiled=True)
+    stack = jnp.stack([amplitudes] * lax.axis_size("col"))
+    gathered = jnp.concatenate(lax.all_to_all(stack, "col", 0, 0), axis=1)
     gathered = gathered * amp_mask(labels_k, irrep_virtual, labels_x)
     masked = lax.all_gather(integrals, "row", axis=1, tiled=True) * int_mask(
         labels_k, irrep_virtual, labels_j, irrep_virtual

time: 220 us -> 323 us (1.47)
  waiting for transfers between devices: 164 us -> 249 us
  starting transfers between devices: 0.08 us -> 10.2 us
  local copies, waits for them, and re-layouts: 2.25 us -> 11.7 us
  matrix products: 29.5 us -> 25.7 us
    all_to_all x0 -> x1, waiting for transfers between devices: none -> 139 us  [per_device(): gathered = jnp.concatenate(lax.all_to_all(stack, 'col', 0, 0), axis=1)]
    all_gather x1 -> x0, waiting for transfers between devices: 55.5 us -> none  [per_device(): gathered = lax.all_gather(amplitudes, 'col', axis=1, tiled=True)]
    all_to_all x0 -> x1, starting transfers between devices: none -> 10.1 us  [per_device(): gathered = jnp.concatenate(lax.all_to_all(stack, 'col', 0, 0), axis=1)]
    another operation x0 -> x1, local copies, waits for them, and re-layouts: none -> 5.9 us  [per_device(): stack = jnp.stack([amplitudes] * lax.axis_size('col'))]
    all_to_all x0 -> x1, local copies, waits for them, and re-layouts: none -> 4.8 us  [per_device(): gathered = jnp.concatenate(lax.all_to_all(stack, 'col', 0, 0), axis=1)]
    mul x0 -> x1, other arithmetic: none -> 4.22 us  [per_device(): gathered = gathered * amp_mask(labels_k, irrep_virtual, labels_x)]
    dot_general x1, matrix products: 29.5 us -> 25.7 us  [contract(): jnp.einsum('kcjb,kcx->jbx', right_int, left_amp, precision=lax.Precision....]
  transfers between devices with their start and end apart: 3 -> 3, of which waited for: 3 -> 3; matrix products, arithmetic and copies ran while one was open for 6% -> 3% of each run, Pallas kernels for 0% -> 0%
where the time goes in v1:
time: 323 us
  waiting for transfers between devices  249 us (77%)
  matrix products  25.7 us (8%)
  between operations  13.5 us (4%)
  other arithmetic  13.3 us (4%)
  local copies, waits for them, and re-layouts  11.7 us (4%)
  starting transfers between devices  10.2 us (3%)
    all_to_all x1, waiting for transfers between devices, per_device(): gathered = jnp.concatenate(lax.all_to_all(stack, 'col', 0, 0), axis=1)  139 us
    all_gather x1, waiting for transfers between devices, per_device(): lax.all_gather(integrals, 'row', axis=1, tiled=True)  56 us
    reduce_scatter x1, waiting for transfers between devices, per_device(): lax.psum_scatter(partial_sum, 'depth', scatter_dimension=1, tiled=True)  53.3 us
    dot_general x1, matrix products, contract(): jnp.einsum('kcjb,kcx->jbx', right_int, left_amp, precision=lax.Precision....  25.7 us
    all_to_all x1, starting transfers between devices, per_device(): gathered = jnp.concatenate(lax.all_to_all(stack, 'col', 0, 0), axis=1)  10.1 us
    mul x1, other arithmetic, per_device(): lax.all_gather(integrals, 'row', axis=1, tiled=True)  8.16 us
  transfers between devices with their start and end apart: 3, of which 3 were waited for; matrix products, arithmetic and copies ran while one was open for 3% of the time, Pallas kernels for 0%

profile of v1, /device:TPU:1, one launch (start us, length us, event | category | flops | bytes accessed | tf_op | source)
XLA Modules:
  0.0 323.2 jit_solution(5010459104413232073)
XLA Ops:
  6.5 5.9 %stack.2 = f32[16,2,48,1536]{3,2,1,0:T(8,128)} broadcast(f32[2,48,1536]{2,1,0:T(8,128)} %param.6), dimensions={1,2,3} | broadcast | bytes 10027008 | tf_op jit(solution)/shard_map/stack | solution.py:40
  12.4 0.0 copy-start
  12.4 0.0 copy-start.1
  12.4 0.0 copy-start.2
  12.4 0.0 copy-start.3
  12.4 10.1 %all-to-all-start = ((f32[16,2,48,1536]{3,2,1,0:T(8,128)}), f32[16,2,48,1536]{3,2,1,0:T(8,128)}, u32[]{:S(2)}, u32[]{:S(2)}) async-start(f32[16,2,48,1536]{3,2,1,0:T(8,128)} %stack.2), calls=%async_computation | async-start | bytes 18874368 | tf_op jit(solution)/shard_map/all_to_all | solution.py:41
  22.6 0.0 all-gather.2.cloned.1.call-start
  22.6 0.7 all-gather.2.cloned.1.call-update
  23.3 0.0 reduce-scatter.2.cloned.1.call-start
  23.3 0.0 copy-done
  23.3 0.0 copy-done.1
  23.4 0.2 broadcast_xor_fusion
  23.5 0.2 xor.105
  23.7 0.1 dynamic_slice.11
  23.8 0.0 copy-done.2
  23.8 0.1 dynamic_slice.9
  23.9 0.0 copy-done.3
  23.9 0.6 dynamic_slice.10
  24.5 0.6 broadcast_xor_fusion.2
  25.1 0.1 broadcast_xor_fusion.1
  25.2 56.0 %all-gather.2.cloned.1.call-done = f32[2,768,1,768]{3,2,1,0:T(1,128)} async-done(((f32[2,192,1,768]{3,2,1,0:T(1,128)}), f32[2,768,1,768]{3,2,1,0:T(1,128)}) %all-gather.2.cloned.1.call-update) | async-done | bytes 4718608 | tf_op jit(solution)/shard_map/all_gather | solution.py:43
  81.2 8.2 %compare_select_fusion = f32[2,768,1,768]{3,2,1,0:T(1,128)} fusion(f32[2,768,1,768]{3,2,1,0:T(1,128)} %all-gather.2.cloned.1.call-done, s32[768]{0:T(1024)S(1)} %broadcast_xor_fusion.2, s32[2,768]{1,0:T(2,128)S(1)} %broadcast_xor_fusion.1), kind=kLoop, calls=%fused_computation | loop fusion | flops 3538944 | bytes 9446400 | tf_op jit(solution)/shard_map/mul | solution.py:43
  89.3 139.1 %all-to-all-done = f32[16,2,48,1536]{3,2,1,0:T(8,128)} async-done(((f32[16,2,48,1536]{3,2,1,0:T(8,128)}), f32[16,2,48,1536]{3,2,1,0:T(8,128)}, u32[]{:S(2)}, u32[]{:S(2)}) %all-to-all-start) | async-done | bytes 9437216 | tf_op jit(solution)/shard_map/all_to_all | solution.py:41
  228.4 0.0 slice-start
  228.4 4.8 %copy.10 = f32[16,2,48,1536]{3,2,0,1:T(8,128)S(1)} copy(f32[16,2,48,1536]{3,2,1,0:T(8,128)} %all-to-all-done) | data formatting | bytes 18874368 | tf_op jit(solution)/shard_map/all_to_all | solution.py:41
  233.2 0.0 slice-start.1
  233.2 4.2 %bitcast_select_fusion = f32[2,768,1536]{2,1,0:T(8,128)} fusion(f32[16,2,48,1536]{3,2,0,1:T(8,128)S(1)} %copy.10, s32[1536]{0:T(1024)S(1)} %dynamic_slice.11, s32[2,768]{1,0:T(2,128)S(1)} %broadcast_xor_fusion.1), kind=kLoop, calls=%fused_computation.1 | loop fusion | flops 7077888 | bytes 18886656 | tf_op jit(solution)/shard_map/mul | solution.py:42
  237.4 0.0 slice-done
  237.4 0.0 slice-done.1
  237.4 25.7 %fusion.3 = f32[1,768,1536]{2,1,0:T(8,128)} fusion(f32[2,768,1536]{2,1,0:T(8,128)} %bitcast_select_fusion, f32[2,768,1,768]{3,2,1,0:T(1,128)S(1)} %bitcast.16), kind=kOutput, calls=%fused_computation.6 | convolution fusion | flops 21743271936 | bytes 18874368 | tf_op jit(solution)/shard_map/kcjb,kcx->jbx/dot_general | solution.py:23
  263.1 0.0 reduce-scatter.2.cloned.1.call-update
  263.1 53.3 %reduce-scatter.2.cloned.1.call-done = f32[1,192,1536]{2,1,0:T(8,128)} async-done(((f32[1,768,1536]{2,1,0:T(8,128)}), f32[1,192,1536]{2,1,0:T(8,128)}) %reduce-scatter.2.cloned.1.call-update) | async-done | bytes 1179664 | tf_op jit(solution)/shard_map/reduce_scatter | solution.py:47
  (1 shorter events, 0.0 us)
Async XLA Ops:
  12.4 10.9 %copy-start = (s32[768]{0:T(1024)S(1)}, s32[768]{0:T(1024)}, u32[]{:S(2)}) copy-start(s32[768]{0:T(1024)} %param.8) | copy-start | bytes 9220
  12.4 10.9 %copy-start.1 = (s32[8]{0:T(128)S(1)}, s32[8]{0:T(128)}, u32[]{:S(2)}) copy-start(s32[8]{0:T(128)} %param.9) | copy-start | bytes 100
  12.4 11.4 %copy-start.2 = (s32[8]{0:T(128)S(1)}, s32[8]{0:T(128)}, u32[]{:S(2)}) copy-start(s32[8]{0:T(128)} %param.10) | copy-start | bytes 100
  12.4 11.5 %copy-start.3 = (s32[16]{0:T(128)S(1)}, s32[16]{0:T(128)}, u32[]{:S(2)}) copy-start(s32[16]{0:T(128)} %param.11) | copy-start | bytes 196
  12.4 215.9 %all-to-all-start = ((f32[16,2,48,1536]{3,2,1,0:T(8,128)}), f32[16,2,48,1536]{3,2,1,0:T(8,128)}, u32[]{:S(2)}, u32[]{:S(2)}) async-start(f32[16,2,48,1536]{3,2,1,0:T(8,128)} %stack.2), calls=%async_computation | async-start | bytes 18874368 | tf_op jit(solution)/shard_map/all_to_all | solution.py:41
  22.6 58.6 %all-gather.2.cloned.1.call-start = ((), (), s32[]{:S(2)}) async-start(), calls=%async_computation.2 | async-start | bytes 5898240 | tf_op jit(solution)/shard_map/all_gather | solution.py:43
  23.3 293.1 %reduce-scatter.2.cloned.1.call-start = ((), (), s32[]{:S(2)}) async-start(), calls=%async_computation.3 | async-start | bytes 5898240 | tf_op jit(solution)/shard_map/reduce_scatter | solution.py:47
  228.4 9.0 %slice-start = ((s8[4718592]{0:T(1024)(128)(4,1)}), s8[4194304]{0:T(1024)(128)(4,1)S(1)}, s32[]{:S(2)}) async-start(s8[4718592]{0:T(1024)(128)(4,1)} %bitcast.15), calls=%async_computation.4 | async-start | bytes 8388608
  233.2 4.2 %slice-start.1 = ((s8[4718592]{0:T(1024)(128)(4,1)}), s8[524288]{0:T(1024)(128)(4,1)S(1)}, s32[]{:S(2)}) async-start(s8[4718592]{0:T(1024)(128)(4,1)} %bitcast.15), calls=%async_computation.5 | async-start | bytes 1048576
Sparse Core Ops, SparseCore 0:
  25.2 55.9 all-gather.1
  263.2 53.0 reduce-scatter.1
